TPU v7x, 512 devices: a whole 4x4x16 slice. The times are simulated.
512 devices in a mesh: blk: 64 (over z_hi, y, x, core), grp: 8 (over z_lo).
Axes of the slice: x: 4, y: 4, z: 16 (z_hi: 2, z_lo: 8; z = z_hi * 8 + z_lo), core: 2. Of those that a mesh axis runs over, the one named last changes fastest.
Arguments:
- samples: float32 [32, 16384], P(None, ('blk', 'grp')), may hold values from 0 to 256
- bounds: int32 [2, 32, 8192], P(None, None, 'blk'), may hold values from 0 to 256, as said below
- spread: float32 [32], replicated, may hold values from 2 to 8
- counts: int32 [8192], P('blk'), may hold values from 0 to 2047
Outputs:
- log_estimate: float32 [8192], P('blk')
- spread_grad: float32 [32], replicated
Inputs may be any that keep to these rules, and one draw needn't show every extreme that they name: For every query and dimension bounds[0] < bounds[1]; each query restricts exactly 3 dimensions to a width of 16 to 48 cells and has bounds 0 and 256 in all others.
All inputs are finite; a program needn't handle non-finite values.
Results may differ from a plain program's by a relative error of at most 0.0003.
Values sent between devices are 32-bit elements; how exact they have to be, the bound alone decides.
A program may use at most 64 MiB of HBM per device.

v0:
```python
import math

import jax
import jax.numpy as jnp
from jax import lax
from jax.sharding import PartitionSpec as P

TABLE_ROWS = 1048576


root_half = 0.7071067811865476
density_norm = 0.3989422804014327


def box_terms(lower_edge, upper_edge, points, inverse):
    upper_arg = (upper_edge - points) * inverse
    lower_arg = (lower_edge - points) * inverse
    in_box = 0.5 * (lax.erf(upper_arg * root_half) - lax.erf(lower_arg * root_half))
    slopes = density_norm * (
        lower_arg * jnp.exp(-0.5 * lower_arg * lower_arg)
        - upper_arg * jnp.exp(-0.5 * upper_arg * upper_arg)
    )
    prefix_prod = jnp.cumprod(in_box, axis=0)
    behind = jnp.flip(jnp.cumprod(jnp.flip(in_box, 0), axis=0), 0)
    unit_row = jnp.ones_like(in_box[:1])
    before = jnp.concatenate([unit_row, prefix_prod[:-1]], 0)
    after_dims = jnp.concatenate([behind[1:], unit_row], 0)
    return (prefix_prod[-1], before * after_dims * slopes)


def finish(est_sum, counts_float, sample_total, query_total):
    smoothing = 1.0 / TABLE_ROWS
    estimate = est_sum / sample_total
    log_est = jnp.log(estimate + smoothing)
    target = jnp.log(counts_float / TABLE_ROWS + smoothing)
    weight = 2.0 * (log_est - target) / (query_total * (estimate + smoothing))
    return (log_est, weight)


def on_device(samples, bounds, spread, counts):
    inverse = 1.0 / spread
    lower_edge = bounds[0].astype(jnp.float32)
    upper_edge = bounds[1].astype(jnp.float32)
    dims = samples.shape[0]
    local_queries = bounds.shape[2]
    sample_total = samples.shape[1] * lax.axis_size("blk") * lax.axis_size("grp")
    query_total = local_queries * lax.axis_size("blk")
    initial = (
        jnp.zeros((local_queries,), jnp.float32),
        jnp.zeros((dims, local_queries), jnp.float32),
    )
    piece = lax.all_gather(samples, "blk", axis=1, tiled=True)
    row_count = piece.shape[1]
    width_rows = math.gcd(row_count, 32)
    blocks = piece.reshape(dims, row_count // width_rows, width_rows).transpose(1, 0, 2)

    def advance(inner, points):
        totals, gradients = box_terms(
            lower_edge[:, :, None],
            upper_edge[:, :, None],
            points[:, None, :],
            inverse[:, None, None],
        )
        return ((inner[0] + totals.sum(axis=1), inner[1] + gradients.sum(axis=2)), None)

    est_sum, grad_sum = lax.scan(advance, initial, blocks)[0]
    est_sum, grad_sum = lax.psum((est_sum, grad_sum), "grp")
    log_est, weight = finish(est_sum, counts.astype(jnp.float32), sample_total, query_total)
    share = jnp.dot(grad_sum, weight, precision=lax.Precision.HIGHEST) / sample_total
    gradient = lax.psum(share, "blk")
    return (log_est, gradient)


def solution(mesh):
    return jax.shard_map(
        on_device,
        mesh=mesh,
        in_specs=(P(None, ("blk", "grp")), P(None, None, "blk"), P(), P("blk")),
        out_specs=(P("blk"), P()),
        check_vma=False,
    )
```

profile of v0, /device:TPU:1, one launch (start us, length us, event | category | flops | bytes accessed | tf_op | source)
XLA Modules:
  0.0 701.9 jit_solution(682669079754419878)
XLA Ops:
  2.1 168.5 %all_gather.3 = f32[32,2048]{0,1:T(8,128)S(1)} all-gather(f32[32,32]{0,1:T(8,128)S(1)} %copy.7), channel_id=1, replica_groups=mesh['blk'=64,'grp'=8] {'blk'}, dimensions={1}, use_global_device_ids=true | all-gather | bytes 266240 | tf_op jit(solution)/shard_map/all_gather | solution.py:52
  170.6 199.7 %while.13 = (s32[]{:T(128)}, f32[128]{0:T(128)S(1)}, f32[32,128]{1,0:T(8,128)S(1)}, f32[32,128]{1,0:T(8,128)S(1)}, f32[64,32,32]{1,2,0:T(8,128)S(1)}, /*index=5*...) while((s32[]{:T(128)}, f32[128]{0:T(128)S(1)}, f32[32,128]{1,0:T(8,128)S(1)}, ...), condition=%wide.region_5.6_spmd.clone, body=%wide.region_0.5_spmd.clone.sunk | while | flops 12198019 | bytes 10025512 | solution.py:66
  172.2 1.0 slice-done
  175.4 1.0 slice-done
  178.5 1.0 slice-done
  181.6 1.0 slice-done
  184.7 1.0 slice-done
  187.9 1.0 slice-done
  191.0 1.0 slice-done
  194.1 1.0 slice-done
  197.2 1.0 slice-done
  200.3 1.0 slice-done
  203.5 1.0 slice-done
  206.6 1.0 slice-done
  209.7 1.0 slice-done
  212.8 1.0 slice-done
  215.9 1.0 slice-done
  219.1 1.0 slice-done
  222.2 1.0 slice-done
  225.3 1.0 slice-done
  228.4 1.0 slice-done
  231.5 1.0 slice-done
  237.8 1.0 slice-done
  240.9 1.0 slice-done
  247.1 1.0 slice-done
  250.3 1.0 slice-done
  259.6 1.0 slice-done
  269.0 1.0 slice-done
  278.3 1.0 slice-done
  281.5 1.0 slice-done
  287.7 1.0 slice-done
  290.8 1.0 slice-done
  297.1 1.0 slice-done
  300.2 1.0 slice-done
  306.4 1.0 slice-done
  309.6 1.0 slice-done
  318.9 1.0 slice-done
  328.3 1.0 slice-done
  337.6 1.0 slice-done
  340.8 1.0 slice-done
  347.0 1.0 slice-done
  350.1 1.0 slice-done
  356.4 1.0 slice-done
  359.5 1.0 slice-done
  365.7 1.0 slice-done
  368.8 1.0 slice-done
  370.3 45.3 %all-reduce.2 = (f32[128]{0:T(128)S(1)}, f32[32,128]{1,0:T(8,128)S(1)}) all-reduce(f32[128]{0:T(128)S(1)} %get-tuple-element.40, f32[32,128]{1,0:T(8,128)S(1)} %get-tuple-element.41), channel_id=1, replica_groups=mesh['blk'=64,'grp'=8] {'grp'}, use_global_device_ids=true, to_apply=%region_6.7 | all-reduce | flops 4224 | bytes 33792 | tf_op jit(solution)/shard_map/psum | solution.py:67
  416.7 285.1 %psum.23 = f32[32]{0:T(128)} all-reduce(f32[32]{0:T(128)S(1)} %fusion.18), channel_id=1, replica_groups=mesh['blk'=64,'grp'=8] {'blk'}, use_global_device_ids=true, to_apply=%region_8.9 | all-reduce | flops 32 | bytes 256 | tf_op jit(solution)/shard_map/psum | solution.py:70
  (995 shorter events, 152.7 us)
Async XLA Ops:
  0.6 1.4 copy-start.1
  172.2 1.0 slice-start
  175.3 1.0 slice-start
  178.4 1.0 slice-start
  181.6 1.0 slice-start
  184.7 1.0 slice-start
  187.8 1.0 slice-start
  190.9 1.0 slice-start
  194.0 1.0 slice-start
  197.2 1.0 slice-start
  200.3 1.0 slice-start
  203.4 1.0 slice-start
  206.5 1.0 slice-start
  209.6 1.0 slice-start
  212.8 1.0 slice-start
  215.9 1.0 slice-start
  219.0 1.0 slice-start
  222.1 1.0 slice-start
  225.2 1.0 slice-start
  228.4 1.0 slice-start
  231.5 1.0 slice-start
  234.6 1.0 slice-start
  237.7 1.0 slice-start
  240.8 1.0 slice-start
  244.0 1.0 slice-start
  247.1 1.0 slice-start
  250.2 1.0 slice-start
  253.3 1.0 slice-start
  256.4 1.0 slice-start
  259.6 1.0 slice-start
  262.7 1.0 slice-start
  265.8 1.0 slice-start
  268.9 1.0 slice-start
  272.1 1.0 slice-start
  278.3 1.0 slice-start
  287.7 1.0 slice-start
  297.0 1.0 slice-start
  300.1 1.0 slice-start
  306.4 1.0 slice-start
  309.5 1.0 slice-start
  318.9 1.0 slice-start
  328.2 1.0 slice-start
  337.6 1.0 slice-start
  346.9 1.0 slice-start
  356.3 1.0 slice-start
  359.4 1.0 slice-start
  365.7 1.0 slice-start
  368.8 1.0 slice-start
  (84 other events, 70.0 us)
where the time goes:
time: 705 us; the launch traced here: 702 us
  blocking collectives  499 us (71%)
  local copies, waits for them, and re-layouts  126 us (18%)
  other arithmetic  69.8 us (10%)
    psum x1, blocking collectives, on_device(): gradient = lax.psum(share, 'blk')  285 us
    all_gather x1, blocking collectives, on_device(): piece = lax.all_gather(samples, 'blk', axis=1, tiled=True)  169 us
    slice x128, local copies, waits for them, and re-layouts, box_terms(): before = jnp.concatenate([unit_row, prefix_prod[:-1]], 0)  63.2 us
    while x128, local copies, waits for them, and re-layouts  48.7 us
    psum x1, blocking collectives, on_device(): est_sum, grad_sum = lax.psum((est_sum, grad_sum), 'grp')  45.3 us
    reduce_sum x64, other arithmetic, advance(): gradients.sum(axis=2)  28.5 us
    another operation x64, other arithmetic, box_terms(): prefix_prod = jnp.cumprod(in_box, axis=0)  18.5 us
    sub x64, other arithmetic, box_terms(): lax.erf(upper_arg * root_half) - lax.erf(lower_arg * root_half)  17.2 us

commit v1 on v0

v1 whole, which is shorter than its diff:
```python
import functools
import math

import jax
import jax.numpy as jnp
from jax import lax
from jax.experimental import pallas as pl
from jax.experimental.pallas import tpu as pltpu
from jax.sharding import PartitionSpec as P

TABLE_ROWS = 1048576
MESH = pl.DeviceIdType.MESH
F32 = jnp.float32
BF16 = jnp.bfloat16

UNIT = math.sqrt(math.log2(math.e) / 2.0)
LOG2E = math.log2(math.e)
ERF_COEFS = (
    0.939437726891315,
    0.059304200409920856,
    -7.37546114627212e-05,
    -0.00017348738576916883,
    1.7241095109019066e-05,
    -7.97342195757559e-07,
    1.4676678471795133e-08,
)
SLOPE_SCALE = 2.0 / (math.sqrt(2.0 * math.pi) * UNIT)

GRID = 256
ROWS_PER_HALF = 7 * 128
DEPTH = 208


def erf_and_moment(v):
    w = v * v
    poly = jnp.full_like(w, ERF_COEFS[-1])
    for coef in ERF_COEFS[-2::-1]:
        poly = poly * w + coef
    return jnp.tanh(v * poly), v * jnp.exp2(-w)


def split3(x):
    high = x.astype(BF16)
    rest = x - high.astype(F32)
    middle = rest.astype(BF16)
    low = (rest - middle.astype(F32)).astype(BF16)
    return high, middle, low


def dot(a, b, a_dim, b_dim):
    return lax.dot_general(
        a, b, (((a_dim,), (b_dim,)), ((), ())), preferred_element_type=F32
    )


def row_sums(x):
    ones = jnp.ones((8, x.shape[1]), BF16)
    total = None
    for piece in split3(x):
        term = dot(ones, piece, 1, 1)
        total = term if total is None else total + term
    return total[:1]


def kernel(
    sizes,
    sample_total,
    query_total,
    samples_ref,
    bounds_ref,
    spread_ref,
    counts_ref,
    log_ref,
    grad_ref,
    table,
    pieces,
    chosen,
    args,
    inside,
    slopes,
    sums,
    est,
    grad_z,
    grad_a,
    grad_y,
    table_sems,
    a_sems,
    y_sems,
    est_sems,
    gz_sems,
    ga_sems,
    gy_sems,
):
    n_hi, n_y, n_a, n_lo = sizes
    n_z = n_hi * n_lo
    dims = samples_ref.shape[0]
    width = samples_ref.shape[1] * n_a
    blk = lax.axis_index("blk")
    z_lo = lax.axis_index("grp")
    z_hi = blk // (n_y * n_a)
    y = (blk // n_a) % n_y
    a = blk % n_a
    z = z_hi * n_lo + z_lo

    def at_z(step):
        other = (z + step) % n_z
        return ((other // n_lo) * (n_y * n_a) + y * n_a + a, other % n_lo)

    def at_a(step):
        return (z_hi * (n_y * n_a) + y * n_a + (a + step) % n_a, z_lo)

    def at_y(step):
        return (z_hi * (n_y * n_a) + ((y + step) % n_y) * n_a + a, z_lo)

    partner = ((1 - z_hi) * (n_y * n_a) + y * n_a + a, z_lo)

    barrier = pltpu.get_barrier_semaphore()
    peers = [at_z(i) for i in range(1, n_z)]
    peers += [at_a(i) for i in range(1, n_a)]
    peers += [at_y(i) for i in range(1, n_y)]
    for peer in peers:
        pl.semaphore_signal(barrier, inc=1, device_id=peer, device_id_type=MESH)

    def send(src, dst, sems, slot, peer):
        copy = pltpu.make_async_remote_copy(
            src_ref=src,
            dst_ref=dst,
            send_sem=sems.at[0, slot],
            recv_sem=sems.at[1, slot],
            device_id=peer,
            device_id_type=MESH,
        )
        copy.start()
        return copy

    x = samples_ref[...]
    pieces[y, a] = jnp.concatenate(
        [x[8 * i : 8 * i + 8] for i in range(dims // 8)], axis=1
    )
    inverse = UNIT / spread_ref[...]
    eye = lax.broadcasted_iota(jnp.int32, (dims, dims), 0) == lax.broadcasted_iota(
        jnp.int32, (dims, dims), 1
    )
    inverse = jnp.sum(jnp.where(eye, inverse, 0.0), axis=1, keepdims=True)
    lower = bounds_ref[0]
    upper = bounds_ref[1]
    restricted = (upper - lower) < GRID
    below = lax.broadcasted_iota(jnp.int32, (dims, dims), 0) > lax.broadcasted_iota(
        jnp.int32, (dims, dims), 1
    )
    rank = dot(
        jnp.where(below, 1.0, 0.0).astype(BF16),
        jnp.where(restricted, 1.0, 0.0).astype(BF16),
        1,
        0,
    )
    dim_ids = lax.broadcasted_iota(jnp.int32, (dims, 128), 0).astype(F32)
    scaled_upper = upper.astype(F32) * inverse
    scaled_lower = lower.astype(F32) * inverse
    rows = []
    for k in range(3):
        mine = restricted & (rank == float(k))
        for values in (scaled_upper, scaled_lower, dim_ids):
            rows.append(
                jnp.sum(jnp.where(mine, values, 0.0), axis=0, keepdims=True)
            )
    rows.append(counts_ref[...].astype(F32))
    rows.append(jnp.zeros((6, 128), F32))
    table[z_hi] = jnp.concatenate(rows, axis=0)

    pl.semaphore_wait(barrier, len(peers))

    copies = []
    a_copies = [
        send(pieces.at[y, a], pieces.at[y, a], a_sems, i - 1, at_a(i))
        for i in range(1, n_a)
    ]
    table_copy = send(table.at[z_hi], table.at[z_hi], table_sems, 0, partner)

    sums[...] = jnp.zeros_like(sums)

    def hot_rows(half):
        values = table[half]
        return [
            jnp.where(dim_ids == values[3 * k + 2 : 3 * k + 3], 1.0, 0.0)
            for k in range(3)
        ]

    def choose(half):
        values = table[half]
        hots = hot_rows(half)
        free = 1.0 - (hots[0] + hots[1] + hots[2])
        nothing = jnp.zeros((3 * dims, 128), BF16)
        pad = jnp.zeros((13, 128), F32)
        for k in range(3):
            minus = -hots[k].astype(BF16)
            for side in range(2):
                edge = values[3 * k + side : 3 * k + side + 1]
                high = edge.astype(BF16).astype(F32)
                middle = (edge - high).astype(BF16).astype(F32)
                low = edge - high - middle
                ends = jnp.concatenate([high, middle, low, pad], axis=0)
                column = (2 * k + side) * 128
                chosen[half, :, column : column + 128] = jnp.concatenate(
                    [minus, minus, minus, nothing, ends.astype(BF16)], axis=0
                )
        free = free.astype(BF16)
        offset = jnp.concatenate(
            [jnp.full((1, 128), -3.0, F32), jnp.zeros((15, 128), F32)], axis=0
        )
        chosen[half, :, 6 * 128 :] = jnp.concatenate(
            [nothing, free, free, free, offset.astype(BF16)], axis=0
        )

    choose(z_hi)
    row = lax.broadcasted_iota(jnp.int32, (16, width), 0)
    ones = jnp.where(row < 3, 1.0, 0.0).astype(BF16)

    def prepare(chunk):
        tiles = [pieces[chunk, i] for i in range(n_a)]
        step = samples_ref.shape[1]
        points = jnp.concatenate(
            [
                jnp.concatenate(
                    [t[:, step * i : step * i + step] for t in tiles], axis=1
                )
                for i in range(dims // 8)
            ],
            axis=0,
        )
        v_low = -points * inverse
        v_high = float(GRID) * inverse + v_low
        erf_high, moment_high = erf_and_moment(v_high)
        erf_low, moment_low = erf_and_moment(v_low)
        double_mass = erf_high - erf_low
        slopes[chunk] = (moment_low - moment_high) / double_mass
        logs = jnp.log(0.5 * double_mass) * LOG2E
        return jnp.concatenate(
            list(split3(-v_low)) + list(split3(logs)) + [ones], axis=0
        )

    def work(chunk, half, right):
        args[...] = dot(chosen[half], right, 0, 0)

        def tile(i, carry):
            start = pl.multiple_of(i * 8, 8)
            masses, moments = [], []
            for k in range(3):
                erf_high, moment_high = erf_and_moment(
                    args[pl.ds(start + 2 * k * 128, 8), :]
                )
                erf_low, moment_low = erf_and_moment(
                    args[pl.ds(start + (2 * k + 1) * 128, 8), :]
                )
                masses.append(erf_high - erf_low)
                moments.append(moment_low - moment_high)
            rest = jnp.exp2(args[pl.ds(start + 6 * 128, 8), :])
            rest0 = rest * masses[0]
            rest01 = rest0 * masses[1]
            within = rest01 * masses[2]
            inside[chunk, half, pl.ds(start, 8), :] = within
            parts = [
                within,
                rest * (masses[1] * masses[2]) * moments[0],
                rest0 * masses[2] * moments[1],
                rest01 * moments[2],
            ]
            for n, part in enumerate(parts):
                folded = part[:, :128]
                for j in range(1, width // 128):
                    folded = folded + part[:, 128 * j : 128 * j + 128]
                sums[n, half, pl.ds(start, 8), :] += folded
            return carry

        lax.fori_loop(0, 128 // 8, tile, 0, unroll=2)

    for copy in a_copies:
        copy.wait_recv()
    y_copies = [
        send(pieces.at[y], pieces.at[y], y_sems, i - 1, at_y(i)) for i in range(1, n_y)
    ]
    right = prepare(y)
    work(y, z_hi, right)
    table_copy.wait_recv()
    choose(1 - z_hi)
    work(y, 1 - z_hi, right)
    for i in range(1, n_y):
        y_copies[i - 1].wait_recv()
        chunk = (y + n_y - i) % n_y
        right = prepare(chunk)
        work(chunk, z_hi, right)
        work(chunk, 1 - z_hi, right)

    for half in range(n_hi):
        est[z, half : half + 1] = row_sums(sums[0, half])
    est_copies = [
        send(est.at[z], est.at[z], est_sems, i - 1, at_z(i)) for i in range(1, n_z)
    ]
    derivs = []
    for half in range(n_hi):
        hots = hot_rows(half)
        free = 1.0 - (hots[0] + hots[1] + hots[2])
        total = jnp.zeros((dims, 128), F32)
        for chunk in range(n_y):
            steep, steep_rest, _ = split3(slopes[chunk])
            within, within_rest, _ = split3(inside[chunk, half])
            total = total + dot(steep, within, 1, 1)
            total = total + dot(steep_rest, within, 1, 1)
            total = total + dot(steep, within_rest, 1, 1)
        total = total * free
        for k in range(3):
            total = total + hots[k] * row_sums(sums[k + 1, half])
        derivs.append(total)
    for copy in est_copies:
        copy.wait_recv()
    smoothing = 1.0 / TABLE_ROWS
    estimate = est[0]
    for i in range(1, n_z):
        estimate = estimate + est[i]
    estimate = estimate / sample_total
    counts = jnp.concatenate([table[half][9:10] for half in range(n_hi)], axis=0)
    log_est = jnp.log(estimate + smoothing)
    target = jnp.log(counts / TABLE_ROWS + smoothing)
    weight = 2.0 * (log_est - target) / (query_total * (estimate + smoothing))
    log_ref[...] = jnp.where(z_hi == 0, log_est[0:1], log_est[1:2])
    weighted = derivs[0] * weight[0:1]
    for half in range(1, n_hi):
        weighted = weighted + derivs[half] * weight[half : half + 1]
    weighted = jnp.concatenate([weighted, jnp.zeros((128 - dims, 128), F32)], axis=0)
    share = row_sums(weighted) * (SLOPE_SCALE / sample_total)

    def reduce_over(value, buffer, sems, place, peers):
        buffer[place] = value
        started = [
            send(buffer.at[place], buffer.at[place], sems, i, peer)
            for i, peer in enumerate(peers)
        ]
        for copy in started:
            copy.wait_recv()
        total = buffer[0]
        for i in range(1, buffer.shape[0]):
            total = total + buffer[i]
        return total, started

    share, gz = reduce_over(
        share, grad_z, gz_sems, z, [at_z(i) for i in range(1, n_z)]
    )
    share, ga = reduce_over(
        share, grad_a, ga_sems, a, [at_a(i) for i in range(1, n_a)]
    )
    share, gy = reduce_over(
        share, grad_y, gy_sems, y, [at_y(i) for i in range(1, n_y)]
    )
    grad_ref[...] = share[:, :dims]
    for copy in a_copies + [table_copy] + y_copies + est_copies + gz + ga + gy:
        copy.wait_send()


def on_device(sizes, samples, bounds, spread, counts):
    n_hi, n_y, n_a, n_lo = sizes
    n_z = n_hi * n_lo
    dims, local = samples.shape
    width = local * n_a
    queries = bounds.shape[2]
    sample_total = local * n_hi * n_y * n_a * n_lo
    query_total = queries * n_hi * n_y * n_a
    vmem = pl.BlockSpec(memory_space=pltpu.VMEM)
    dma = pltpu.SemaphoreType.DMA
    log_est, grad = pl.pallas_call(
        functools.partial(kernel, sizes, float(sample_total), float(query_total)),
        out_shape=(
            jax.ShapeDtypeStruct((1, queries), F32),
            jax.ShapeDtypeStruct((1, dims), F32),
        ),
        in_specs=[vmem] * 4,
        out_specs=(vmem, vmem),
        scratch_shapes=[
            pltpu.VMEM((n_hi, 16, 128), F32),
            pltpu.VMEM((n_y, n_a, 8, 128), F32),
            pltpu.VMEM((n_hi, DEPTH, ROWS_PER_HALF), BF16),
            pltpu.VMEM((ROWS_PER_HALF, width), F32),
            pltpu.VMEM((n_y, n_hi, 128, width), F32),
            pltpu.VMEM((n_y, dims, width), F32),
            pltpu.VMEM((4, n_hi, 128, 128), F32),
            pltpu.VMEM((n_z, n_hi, 128), F32),
            pltpu.VMEM((n_z, 1, 128), F32),
            pltpu.VMEM((n_a, 1, 128), F32),
            pltpu.VMEM((n_y, 1, 128), F32),
            dma((2, 1)),
            dma((2, n_a - 1)),
            dma((2, n_y - 1)),
            dma((2, n_z - 1)),
            dma((2, n_z - 1)),
            dma((2, n_a - 1)),
            dma((2, n_y - 1)),
        ],
        compiler_params=pltpu.CompilerParams(
            collective_id=0, has_side_effects=True, vmem_limit_bytes=40 * 1024 * 1024
        ),
    )(samples, bounds, spread.reshape(1, dims), counts.reshape(1, queries))
    return log_est.reshape(queries), grad.reshape(dims)


def solution(mesh):
    n_blk = mesh.shape["blk"]
    sizes = (2, 4, n_blk // 8, mesh.shape["grp"])
    return jax.shard_map(
        functools.partial(on_device, sizes),
        mesh=mesh,
        in_specs=(P(None, ("blk", "grp")), P(None, None, "blk"), P(), P("blk")),
        out_specs=(P("blk"), P()),
        check_vma=False,
    )
```

time: 705 us -> 56.5 us (0.08)
  blocking collectives: 499 us -> 0 us
  local copies, waits for them, and re-layouts: 126 us -> 3.15 us
  other arithmetic: 69.8 us -> 0 us
  Pallas kernels: 0 us -> 52.4 us
    psum x2 -> x0, blocking collectives: 330 us -> none  [the longest x1 285 us: on_device(): gradient = lax.psum(share, 'blk')]
    all_gather x1 -> x0, blocking collectives: 169 us -> none  [on_device(): piece = lax.all_gather(samples, 'blk', axis=1, tiled=True)]
    slice x256 -> x0, local copies, waits for them, and re-layouts: 67.6 us -> none  [the longest x128 63.2 us: box_terms(): before = jnp.concatenate([unit_row, prefix_prod[:-1]], 0)]
    pallas_call x0 -> x1, Pallas kernels: none -> 52.4 us  [on_device(): pl.pallas_call(functools.partial(kernel, sizes, float(sample_total), floa...]
    while x128 -> x0, local copies, waits for them, and re-layouts: 48.7 us -> none
    reduce_sum x128 -> x0, other arithmetic: 29.8 us -> none  [the longest x64 28.5 us: advance(): gradients.sum(axis=2)]
    another operation x128 -> x0, other arithmetic: 21.7 us -> none  [the longest x64 18.5 us: box_terms(): prefix_prod = jnp.cumprod(in_box, axis=0)]
    sub x64 -> x0, other arithmetic: 17.2 us -> none  [box_terms(): lax.erf(upper_arg * root_half) - lax.erf(lower_arg * root_half)]
where the time goes in v1:
time: 56.5 us; the launch traced here: 56.3 us
  Pallas kernels  52.4 us (93%)
  local copies, waits for them, and re-layouts  3.15 us (6%)
  between operations  0.66 us (1%)
    pallas_call x1, Pallas kernels, on_device(): pl.pallas_call(functools.partial(kernel, sizes, float(sample_total), floa...  52.4 us
    unnamed x10, local copies, waits for them, and re-layouts  3.15 us

profile of v1, /device:TPU:1, one launch (start us, length us, event | category | flops | bytes accessed | tf_op | source)
XLA Modules:
  0.0 56.3 jit_solution(6524327591309613846)
XLA Ops:
  0.6 0.0 copy-start.2
  0.6 0.0 copy-start.3
  0.7 0.6 %copy-done.2 = f32[32]{0:T(128)S(1)} copy-done((f32[32]{0:T(128)S(1)}, f32[32]{0:T(128)}, u32[]{:S(2)}) %copy-start.2) | copy-done | bytes 152
  1.3 0.0 copy-done.3
  1.3 0.0 copy-start
  1.3 0.8 %copy-done = s32[2,32,128]{2,1,0:T(8,128)S(1)} copy-done((s32[2,32,128]{2,1,0:T(8,128)S(1)}, s32[2,32,128]{2,1,0:T(8,128)}, u32[]{:S(2)}) %copy-start) | copy-done | bytes 32792
  2.1 0.0 copy-start.1
  2.1 0.7 %copy-done.1 = f32[32,32]{1,0:T(8,128)S(1)} copy-done((f32[32,32]{1,0:T(8,128)S(1)}, f32[32,32]{1,0:T(8,128)}, u32[]{:S(2)}) %copy-start.1) | copy-done | bytes 4120
  2.8 52.4 %shard_map.59 = (f32[1,128]{1,0:T(1,128)S(1)}, f32[1,32]{1,0:T(1,128)S(1)}) custom-call(f32[32,32]{1,0:T(8,128)S(1)} %copy-done.1, s32[2,32,128]{2,1,0:T(8,128)S(1)} %copy-done, f32[1,32]{1,0:T(1,128)S(1)} %bitcast.4, s32[1,128]{1,0:T(1,128)S(1)} %bitcast.5), custom_call_target="tpu_custom_call" | custom-call | tf_op jit(solution)/shard_map/pallas_call | solution.py:369
  55.2 0.5 copy.8
  55.7 0.5 copy.9
Async XLA Ops:
  0.6 0.7 %copy-start.2 = (f32[32]{0:T(128)S(1)}, f32[32]{0:T(128)}, u32[]{:S(2)}) copy-start(f32[32]{0:T(128)} %param.6) | copy-start | bytes 388
  0.6 0.7 %copy-start.3 = (s32[128]{0:T(128)S(1)}, s32[128]{0:T(128)}, u32[]{:S(2)}) copy-start(s32[128]{0:T(128)} %param.7) | copy-start | bytes 1540
  1.3 0.8 %copy-start = (s32[2,32,128]{2,1,0:T(8,128)S(1)}, s32[2,32,128]{2,1,0:T(8,128)}, u32[]{:S(2)}) copy-start(s32[2,32,128]{2,1,0:T(8,128)} %bounds_ref.1) | copy-start | bytes 98308
  2.1 0.7 %copy-start.1 = (f32[32,32]{1,0:T(8,128)S(1)}, f32[32,32]{1,0:T(8,128)}, u32[]{:S(2)}) copy-start(f32[32,32]{1,0:T(8,128)} %samples_ref.1) | copy-start | bytes 12292

commit v2 on v1

v2 whole, which is shorter than its diff:
```python
import functools
import math

import jax
import jax.numpy as jnp
from jax import lax
from jax.experimental import pallas as pl
from jax.experimental.pallas import tpu as pltpu
from jax.sharding import PartitionSpec as P

TABLE_ROWS = 1048576
MESH = pl.DeviceIdType.MESH
F32 = jnp.float32
BF16 = jnp.bfloat16

UNIT = math.sqrt(math.log2(math.e) / 2.0)
LOG2E = math.log2(math.e)
ERF_COEFS = (
    0.939437726891315,
    0.059304200409920856,
    -7.37546114627212e-05,
    -0.00017348738576916883,
    1.7241095109019066e-05,
    -7.97342195757559e-07,
    1.4676678471795133e-08,
)
SLOPE_SCALE = 2.0 / (math.sqrt(2.0 * math.pi) * UNIT)

GRID = 256
ROWS_PER_HALF = 7 * 128
DEPTH = 208


def erf_and_moment(v):
    w = v * v
    poly = jnp.full_like(w, ERF_COEFS[-1])
    for coef in ERF_COEFS[-2::-1]:
        poly = poly * w + coef
    return jnp.tanh(v * poly), v * jnp.exp2(-w)


def split3(x):
    high = x.astype(BF16)
    rest = x - high.astype(F32)
    middle = rest.astype(BF16)
    low = (rest - middle.astype(F32)).astype(BF16)
    return high, middle, low


def dot(a, b, a_dim, b_dim):
    return lax.dot_general(
        a, b, (((a_dim,), (b_dim,)), ((), ())), preferred_element_type=F32
    )


def row_sums(x):
    pieces = jnp.concatenate(split3(x), axis=1)
    return dot(jnp.ones((8, pieces.shape[1]), BF16), pieces, 1, 1)[:1]


def kernel(
    sizes,
    sample_total,
    query_total,
    samples_hbm,
    bounds_hbm,
    spread_hbm,
    counts_hbm,
    log_ref,
    grad_ref,
    samples_ref,
    bounds_ref,
    spread_ref,
    counts_ref,
    table,
    pieces,
    rights,
    chosen,
    args,
    inside,
    slopes,
    sums,
    est,
    grad_z,
    grad_p,
    input_sems,
    table_sems,
    piece_sends,
    piece_recvs,
    est_sems,
    gz_sems,
    gp_sems,
):
    n_hi, n_y, n_a, n_lo = sizes
    n_z = n_hi * n_lo
    n_p = n_y * n_a
    dims, local = samples_ref.shape
    width = local * n_a

    inputs = []
    for i, (src, dst) in enumerate(
        (
            (samples_hbm, samples_ref),
            (spread_hbm, spread_ref),
            (bounds_hbm, bounds_ref),
            (counts_hbm, counts_ref),
        )
    ):
        copy = pltpu.make_async_copy(src, dst, input_sems.at[i])
        copy.start()
        inputs.append(copy)

    blk = lax.axis_index("blk")
    z_lo = lax.axis_index("grp")
    z_hi = blk // n_p
    plane = blk % n_p
    y = plane // n_a
    a = plane % n_a
    z = z_hi * n_lo + z_lo

    def at_z(step):
        other = (z + step) % n_z
        return ((other // n_lo) * n_p + plane, other % n_lo)

    def at_p(y_step, a_step):
        return (z_hi * n_p + ((y + y_step) % n_y) * n_a + (a + a_step) % n_a, z_lo)

    partner = ((1 - z_hi) * n_p + plane, z_lo)
    plane_steps = [(i, j) for i in range(n_y) for j in range(n_a) if i or j]

    barrier = pltpu.get_barrier_semaphore()
    peers = [at_p(i, j) for i, j in plane_steps]
    peers += [at_z(i) for i in range(1, n_z)]
    for peer in peers:
        pl.semaphore_signal(barrier, inc=1, device_id=peer, device_id_type=MESH)

    def send(ref, send_sem, recv_sem, peer):
        copy = pltpu.make_async_remote_copy(
            src_ref=ref,
            dst_ref=ref,
            send_sem=send_sem,
            recv_sem=recv_sem,
            device_id=peer,
            device_id_type=MESH,
        )
        copy.start()
        return copy

    def wait_bytes(ref, sem):
        pltpu.make_async_copy(ref, ref, sem).wait()

    inputs[0].wait()
    x = samples_ref[...]
    pieces[plane] = jnp.concatenate(
        [x[8 * i : 8 * i + 8] for i in range(dims // 8)], axis=1
    )
    pl.semaphore_wait(barrier, len(peers))
    for i, j in plane_steps:
        send(pieces.at[plane], piece_sends.at[0], piece_recvs.at[i], at_p(i, j))

    inputs[1].wait()
    inverse = UNIT / spread_ref[...]
    eye = lax.broadcasted_iota(jnp.int32, (dims, dims), 0) == lax.broadcasted_iota(
        jnp.int32, (dims, dims), 1
    )
    inverse = jnp.sum(jnp.where(eye, inverse, 0.0), axis=1, keepdims=True)
    inputs[2].wait()
    inputs[3].wait()
    lower = bounds_ref[0]
    upper = bounds_ref[1]
    restricted = (upper - lower) < GRID
    below = lax.broadcasted_iota(jnp.int32, (dims, dims), 0) > lax.broadcasted_iota(
        jnp.int32, (dims, dims), 1
    )
    rank = dot(
        jnp.where(below, 1.0, 0.0).astype(BF16),
        jnp.where(restricted, 1.0, 0.0).astype(BF16),
        1,
        0,
    )
    dim_ids = lax.broadcasted_iota(jnp.int32, (dims, 128), 0).astype(F32)
    scaled_upper = upper.astype(F32) * inverse
    scaled_lower = lower.astype(F32) * inverse
    rows = []
    for k in range(3):
        mine = restricted & (rank == float(k))
        for values in (scaled_upper, scaled_lower, dim_ids):
            rows.append(
                jnp.sum(jnp.where(mine, values, 0.0), axis=0, keepdims=True)
            )
    rows.append(counts_ref[...].astype(F32))
    rows.append(jnp.zeros((6, 128), F32))
    table[z_hi] = jnp.concatenate(rows, axis=0)
    table_copy = send(table.at[z_hi], table_sems.at[0], table_sems.at[1], partner)

    sums[...] = jnp.zeros_like(sums)

    def hot_rows(half):
        values = table[half]
        return [
            jnp.where(dim_ids == values[3 * k + 2 : 3 * k + 3], 1.0, 0.0)
            for k in range(3)
        ]

    def choose(half):
        values = table[half]
        hots = hot_rows(half)
        free = 1.0 - (hots[0] + hots[1] + hots[2])
        nothing = jnp.zeros((3 * dims, 128), BF16)
        pad = jnp.zeros((13, 128), F32)
        for k in range(3):
            minus = -hots[k].astype(BF16)
            for side in range(2):
                edge = values[3 * k + side : 3 * k + side + 1]
                high = edge.astype(BF16).astype(F32)
                middle = (edge - high).astype(BF16).astype(F32)
                low = edge - high - middle
                ends = jnp.concatenate([high, middle, low, pad], axis=0)
                column = (2 * k + side) * 128
                chosen[half, :, column : column + 128] = jnp.concatenate(
                    [minus, minus, minus, nothing, ends.astype(BF16)], axis=0
                )
        free = free.astype(BF16)
        offset = jnp.concatenate(
            [jnp.full((1, 128), -3.0, F32), jnp.zeros((15, 128), F32)], axis=0
        )
        chosen[half, :, 6 * 128 :] = jnp.concatenate(
            [nothing, free, free, free, offset.astype(BF16)], axis=0
        )

    choose(z_hi)
    row = lax.broadcasted_iota(jnp.int32, (16, width), 0)
    ones = jnp.where(row < 3, 1.0, 0.0).astype(BF16)

    def prepare(chunk):
        tiles = [pieces[chunk * n_a + i] for i in range(n_a)]
        points = jnp.concatenate(
            [
                jnp.concatenate(
                    [t[:, local * i : local * i + local] for t in tiles], axis=1
                )
                for i in range(dims // 8)
            ],
            axis=0,
        )
        v_low = -points * inverse
        v_high = float(GRID) * inverse + v_low
        erf_high, moment_high = erf_and_moment(v_high)
        erf_low, moment_low = erf_and_moment(v_low)
        double_mass = erf_high - erf_low
        slopes[chunk] = (moment_low - moment_high) / double_mass
        logs = jnp.log(0.5 * double_mass) * LOG2E
        rights[chunk] = jnp.concatenate(
            list(split3(-v_low)) + list(split3(logs)) + [ones], axis=0
        )

    def block(step, carry):
        i = step % n_y
        chunk = (y + n_y - i) % n_y

        @pl.when(step == 0)
        def _():
            wait_bytes(pieces.at[0 : n_a - 1], piece_recvs.at[i])

        @pl.when((step > 0) & (step < n_y))
        def _():
            wait_bytes(pieces.at[0:n_a], piece_recvs.at[i])

        @pl.when(step < n_y)
        def _():
            prepare(chunk)

        @pl.when(step == n_y)
        def _():
            table_copy.wait_recv()
            choose(1 - z_hi)

        half = jnp.where(step < n_y, z_hi, 1 - z_hi)
        args[...] = dot(chosen[half], rights[chunk], 0, 0)
        for start in range(0, 128, 8):
            masses, moments = [], []
            for k in range(3):
                base = start + 2 * k * 128
                erf_high, moment_high = erf_and_moment(args[base : base + 8, :])
                base = base + 128
                erf_low, moment_low = erf_and_moment(args[base : base + 8, :])
                masses.append(erf_high - erf_low)
                moments.append(moment_low - moment_high)
            rest = jnp.exp2(args[start + 6 * 128 : start + 6 * 128 + 8, :])
            rest0 = rest * masses[0]
            rest01 = rest0 * masses[1]
            within = rest01 * masses[2]
            inside[chunk, half, start : start + 8, :] = within
            parts = [
                within,
                rest * (masses[1] * masses[2]) * moments[0],
                rest0 * masses[2] * moments[1],
                rest01 * moments[2],
            ]
            for n, part in enumerate(parts):
                folded = part[:, :128]
                for j in range(1, width // 128):
                    folded = folded + part[:, 128 * j : 128 * j + 128]
                sums[n, half, start : start + 8, :] += folded
        return carry

    lax.fori_loop(0, n_hi * n_y, block, 0)

    for half in range(n_hi):
        est[z, half : half + 1] = row_sums(sums[0, half])
    for i in range(1, n_z):
        send(est.at[z], est_sems.at[0], est_sems.at[1], at_z(i))
    derivs = []
    for half in range(n_hi):
        hots = hot_rows(half)
        free = 1.0 - (hots[0] + hots[1] + hots[2])
        total = jnp.zeros((dims, 128), F32)
        for chunk in range(n_y):
            steep, steep_rest, _ = split3(slopes[chunk])
            within, within_rest, _ = split3(inside[chunk, half])
            total = total + dot(steep, within, 1, 1)
            total = total + dot(steep_rest, within, 1, 1)
            total = total + dot(steep, within_rest, 1, 1)
        total = total * free
        for k in range(3):
            total = total + hots[k] * row_sums(sums[k + 1, half])
        derivs.append(total)
    smoothing = 1.0 / TABLE_ROWS
    counts = jnp.concatenate([table[half][9:10] for half in range(n_hi)], axis=0)
    target = jnp.log(counts / TABLE_ROWS + smoothing)
    wait_bytes(est.at[0 : n_z - 1], est_sems.at[1])
    estimate = est[0]
    for i in range(1, n_z):
        estimate = estimate + est[i]
    estimate = estimate / sample_total
    log_est = jnp.log(estimate + smoothing)
    weight = 2.0 * (log_est - target) / (query_total * (estimate + smoothing))
    weighted = derivs[0] * weight[0:1]
    for half in range(1, n_hi):
        weighted = weighted + derivs[half] * weight[half : half + 1]
    weighted = jnp.concatenate([weighted, jnp.zeros((128 - dims, 128), F32)], axis=0)
    share = row_sums(weighted) * (SLOPE_SCALE / sample_total)

    grad_z[z] = share
    for i in range(1, n_z):
        send(grad_z.at[z], gz_sems.at[0], gz_sems.at[1], at_z(i))
    log_ref[...] = jnp.where(z_hi == 0, log_est[0:1], log_est[1:2])
    wait_bytes(grad_z.at[0 : n_z - 1], gz_sems.at[1])
    share = grad_z[0]
    for i in range(1, n_z):
        share = share + grad_z[i]
    grad_p[plane] = share
    for i, j in plane_steps:
        send(grad_p.at[plane], gp_sems.at[0], gp_sems.at[1], at_p(i, j))
    table_copy.wait_send()
    flat = n_p - 1
    wait_bytes(pieces.at[0:flat], piece_sends.at[0])
    wait_bytes(est.at[0 : n_z - 1], est_sems.at[0])
    wait_bytes(grad_z.at[0 : n_z - 1], gz_sems.at[0])
    wait_bytes(grad_p.at[0:flat], gp_sems.at[1])
    share = grad_p[0]
    for i in range(1, n_p):
        share = share + grad_p[i]
    grad_ref[...] = share[:, :dims]
    wait_bytes(grad_p.at[0:flat], gp_sems.at[0])


def on_device(sizes, samples, bounds, spread, counts):
    n_hi, n_y, n_a, n_lo = sizes
    n_z = n_hi * n_lo
    dims, local = samples.shape
    width = local * n_a
    queries = bounds.shape[2]
    sample_total = local * n_hi * n_y * n_a * n_lo
    query_total = queries * n_hi * n_y * n_a
    vmem = pl.BlockSpec(memory_space=pltpu.VMEM)
    whole = pl.BlockSpec(memory_space=pl.ANY)
    dma = pltpu.SemaphoreType.DMA
    log_est, grad = pl.pallas_call(
        functools.partial(kernel, sizes, float(sample_total), float(query_total)),
        out_shape=(
            jax.ShapeDtypeStruct((1, queries), F32),
            jax.ShapeDtypeStruct((1, dims), F32),
        ),
        in_specs=[whole] * 4,
        out_specs=(vmem, vmem),
        scratch_shapes=[
            pltpu.VMEM((dims, local), F32),
            pltpu.VMEM((2, dims, queries), jnp.int32),
            pltpu.VMEM((1, dims), F32),
            pltpu.VMEM((1, queries), jnp.int32),
            pltpu.VMEM((n_hi, 16, 128), F32),
            pltpu.VMEM((n_y * n_a, 8, 128), F32),
            pltpu.VMEM((n_y, DEPTH, width), BF16),
            pltpu.VMEM((n_hi, DEPTH, ROWS_PER_HALF), BF16),
            pltpu.VMEM((ROWS_PER_HALF, width), F32),
            pltpu.VMEM((n_y, n_hi, 128, width), F32),
            pltpu.VMEM((n_y, dims, width), F32),
            pltpu.VMEM((4, n_hi, 128, 128), F32),
            pltpu.VMEM((n_z, n_hi, 128), F32),
            pltpu.VMEM((n_z, 1, 128), F32),
            pltpu.VMEM((n_y * n_a, 1, 128), F32),
            dma((4,)),
            dma((2,)),
            dma((1,)),
            dma((n_y,)),
            dma((2,)),
            dma((2,)),
            dma((2,)),
        ],
        compiler_params=pltpu.CompilerParams(
            collective_id=0, has_side_effects=True, vmem_limit_bytes=40 * 1024 * 1024
        ),
    )(samples, bounds, spread.reshape(1, dims), counts.reshape(1, queries))
    return log_est.reshape(queries), grad.reshape(dims)


def solution(mesh):
    n_blk = mesh.shape["blk"]
    sizes = (2, 4, n_blk // 8, mesh.shape["grp"])
    return jax.shard_map(
        functools.partial(on_device, sizes),
        mesh=mesh,
        in_specs=(P(None, ("blk", "grp")), P(None, None, "blk"), P(), P("blk")),
        out_specs=(P("blk"), P()),
        check_vma=False,
    )
```

time: 56.5 us -> 51.6 us (0.913)
  Pallas kernels: 52.4 us -> 47.5 us
    pallas_call x1, Pallas kernels: 52.4 us -> 47.5 us  [on_device(): pl.pallas_call(functools.partial(kernel, sizes, float(sample_total), floa...]
where the time goes in v2:
time: 51.6 us; the launch traced here: 51.3 us
  Pallas kernels  47.5 us (92%)
  local copies, waits for them, and re-layouts  3.15 us (6%)
  between operations  0.66 us (1%)
    pallas_call x1, Pallas kernels, on_device(): pl.pallas_call(functools.partial(kernel, sizes, float(sample_total), floa...  47.5 us
    unnamed x10, local copies, waits for them, and re-layouts  3.15 us

profile of v2, /device:TPU:1, one launch (start us, length us, event | category | flops | bytes accessed | tf_op | source)
XLA Modules:
  0.0 51.3 jit_solution(6300261355816275425)
XLA Ops:
  0.6 0.0 copy-start.2
  0.6 0.0 copy-start.3
  0.7 0.6 %copy-done.2 = f32[32]{0:T(128)S(1)} copy-done((f32[32]{0:T(128)S(1)}, f32[32]{0:T(128)}, u32[]{:S(2)}) %copy-start.2) | copy-done | bytes 152
  1.3 0.0 copy-done.3
  1.3 0.0 copy-start
  1.3 0.8 %copy-done = s32[2,32,128]{2,1,0:T(8,128)S(1)} copy-done((s32[2,32,128]{2,1,0:T(8,128)S(1)}, s32[2,32,128]{2,1,0:T(8,128)}, u32[]{:S(2)}) %copy-start) | copy-done | bytes 32792
  2.1 0.0 copy-start.1
  2.1 0.7 %copy-done.1 = f32[32,32]{1,0:T(8,128)S(1)} copy-done((f32[32,32]{1,0:T(8,128)S(1)}, f32[32,32]{1,0:T(8,128)}, u32[]{:S(2)}) %copy-start.1) | copy-done | bytes 4120
  2.8 47.5 %shard_map.59 = (f32[1,128]{1,0:T(1,128)S(1)}, f32[1,32]{1,0:T(1,128)S(1)}) custom-call(f32[32,32]{1,0:T(8,128)S(1)} %copy-done.1, s32[2,32,128]{2,1,0:T(8,128)S(1)} %copy-done, f32[1,32]{1,0:T(1,128)S(1)} %bitcast.4, s32[1,128]{1,0:T(1,128)S(1)} %bitcast.5), custom_call_target="tpu_custom_call" | custom-call | tf_op jit(solution)/shard_map/pallas_call | solution.py:379
  50.3 0.5 %copy.8 = f32[128]{0:T(128)} copy(f32[128]{0:T(128)S(1)} %bitcast.7) | data formatting | bytes 1024
  50.8 0.5 copy.9
Async XLA Ops:
  0.6 0.7 %copy-start.2 = (f32[32]{0:T(128)S(1)}, f32[32]{0:T(128)}, u32[]{:S(2)}) copy-start(f32[32]{0:T(128)} %param.6) | copy-start | bytes 388
  0.6 0.7 %copy-start.3 = (s32[128]{0:T(128)S(1)}, s32[128]{0:T(128)}, u32[]{:S(2)}) copy-start(s32[128]{0:T(128)} %param.7) | copy-start | bytes 1540
  1.3 0.8 %copy-start = (s32[2,32,128]{2,1,0:T(8,128)S(1)}, s32[2,32,128]{2,1,0:T(8,128)}, u32[]{:S(2)}) copy-start(s32[2,32,128]{2,1,0:T(8,128)} %bounds_hbm.1) | copy-start | bytes 98308
  2.1 0.7 %copy-start.1 = (f32[32,32]{1,0:T(8,128)S(1)}, f32[32,32]{1,0:T(8,128)}, u32[]{:S(2)}) copy-start(f32[32,32]{1,0:T(8,128)} %samples_hbm.1) | copy-start | bytes 12292

commit v3 on v2

--- a/solution.py
+++ b/solution.py
@@ -27,7 +27,8 @@
 SLOPE_SCALE = 2.0 / (math.sqrt(2.0 * math.pi) * UNIT)
 
 GRID = 256
-ROWS_PER_HALF = 7 * 128
+GROUP = 16
+REACH = 4
 DEPTH = 208
 
 
@@ -76,7 +77,6 @@
     pieces,
     rights,
     chosen,
-    args,
     inside,
     slopes,
     sums,
@@ -90,6 +90,7 @@
     est_sems,
     gz_sems,
     gp_sems,
+    ready,
 ):
     n_hi, n_y, n_a, n_lo = sizes
     n_z = n_hi * n_lo
@@ -125,12 +126,14 @@
     def at_p(y_step, a_step):
         return (z_hi * n_p + ((y + y_step) % n_y) * n_a + (a + a_step) % n_a, z_lo)
 
-    partner = ((1 - z_hi) * n_p + plane, z_lo)
+    partner = ((1 - z_hi) * n_p + plane, (z_lo + n_lo // 2) % n_lo)
     plane_steps = [(i, j) for i in range(n_y) for j in range(n_a) if i or j]
 
     barrier = pltpu.get_barrier_semaphore()
     peers = [at_p(i, j) for i, j in plane_steps]
-    peers += [at_z(i) for i in range(1, n_z)]
+    near = [i for i in range(1, n_z) if min(i, n_z - i) <= REACH]
+    hubs = [i for i in near if min(i, n_z - i) == REACH]
+    peers += [at_z(i) for i in near]
     for peer in peers:
         pl.semaphore_signal(barrier, inc=1, device_id=peer, device_id_type=MESH)
 
@@ -155,6 +158,8 @@
         [x[8 * i : 8 * i + 8] for i in range(dims // 8)], axis=1
     )
     pl.semaphore_wait(barrier, len(peers))
+    for i in hubs:
+        pl.semaphore_signal(ready, inc=1, device_id=at_z(i), device_id_type=MESH)
     for i, j in plane_steps:
         send(pieces.at[plane], piece_sends.at[0], piece_recvs.at[i], at_p(i, j))
 
@@ -206,27 +211,26 @@
         values = table[half]
         hots = hot_rows(half)
         free = 1.0 - (hots[0] + hots[1] + hots[2])
-        nothing = jnp.zeros((3 * dims, 128), BF16)
+        nothing = jnp.zeros((3 * dims, 128), F32)
         pad = jnp.zeros((13, 128), F32)
+        blocks = []
         for k in range(3):
-            minus = -hots[k].astype(BF16)
+            minus = -hots[k]
             for side in range(2):
                 edge = values[3 * k + side : 3 * k + side + 1]
                 high = edge.astype(BF16).astype(F32)
                 middle = (edge - high).astype(BF16).astype(F32)
                 low = edge - high - middle
-                ends = jnp.concatenate([high, middle, low, pad], axis=0)
-                column = (2 * k + side) * 128
-                chosen[half, :, column : column + 128] = jnp.concatenate(
-                    [minus, minus, minus, nothing, ends.astype(BF16)], axis=0
-                )
-        free = free.astype(BF16)
-        offset = jnp.concatenate(
-            [jnp.full((1, 128), -3.0, F32), jnp.zeros((15, 128), F32)], axis=0
-        )
-        chosen[half, :, 6 * 128 :] = jnp.concatenate(
-            [nothing, free, free, free, offset.astype(BF16)], axis=0
-        )
+                blocks.append([minus, minus, minus, nothing, high, middle, low, pad])
+        offset = jnp.full((1, 128), -3.0, F32)
+        none = jnp.zeros((15, 128), F32)
+        blocks.append([nothing, free, free, free, offset, none])
+        for n, block in enumerate(blocks):
+            block = jnp.concatenate(block, axis=0).T.astype(BF16)
+            for group in range(128 // GROUP):
+                chosen[half, group, n * GROUP : n * GROUP + GROUP, :] = block[
+                    group * GROUP : group * GROUP + GROUP
+                ]
 
     choose(z_hi)
     row = lax.broadcasted_iota(jnp.int32, (16, width), 0)
@@ -276,21 +280,22 @@
             choose(1 - z_hi)
 
         half = jnp.where(step < n_y, z_hi, 1 - z_hi)
-        args[...] = dot(chosen[half], rights[chunk], 0, 0)
-        for start in range(0, 128, 8):
+        right = rights[chunk]
+        for group in range(128 // GROUP):
+            terms = dot(chosen[half, group], right, 1, 0)
+            terms = [terms[n * GROUP : n * GROUP + GROUP] for n in range(7)]
+            start = group * GROUP
             masses, moments = [], []
             for k in range(3):
-                base = start + 2 * k * 128
-                erf_high, moment_high = erf_and_moment(args[base : base + 8, :])
-                base = base + 128
-                erf_low, moment_low = erf_and_moment(args[base : base + 8, :])
+                erf_high, moment_high = erf_and_moment(terms[2 * k])
+                erf_low, moment_low = erf_and_moment(terms[2 * k + 1])
                 masses.append(erf_high - erf_low)
                 moments.append(moment_low - moment_high)
-            rest = jnp.exp2(args[start + 6 * 128 : start + 6 * 128 + 8, :])
+            rest = jnp.exp2(terms[6])
             rest0 = rest * masses[0]
             rest01 = rest0 * masses[1]
             within = rest01 * masses[2]
-            inside[chunk, half, start : start + 8, :] = within
+            inside[chunk, half, start : start + GROUP, :] = within
             parts = [
                 within,
                 rest * (masses[1] * masses[2]) * moments[0],
@@ -301,13 +306,15 @@
                 folded = part[:, :128]
                 for j in range(1, width // 128):
                     folded = folded + part[:, 128 * j : 128 * j + 128]
-                sums[n, half, start : start + 8, :] += folded
+                sums[n, half, start : start + GROUP, :] += folded
         return carry
 
     lax.fori_loop(0, n_hi * n_y, block, 0)
 
     for half in range(n_hi):
         est[z, half : half + 1] = row_sums(sums[0, half])
+    if hubs:
+        pl.semaphore_wait(ready, len(hubs))
     for i in range(1, n_z):
         send(est.at[z], est_sems.at[0], est_sems.at[1], at_z(i))
     derivs = []
@@ -341,28 +348,28 @@
     weighted = jnp.concatenate([weighted, jnp.zeros((128 - dims, 128), F32)], axis=0)
     share = row_sums(weighted) * (SLOPE_SCALE / sample_total)
 
+    grad_p[plane] = share
+    for i, j in plane_steps:
+        send(grad_p.at[plane], gp_sems.at[0], gp_sems.at[1], at_p(i, j))
+    log_ref[...] = jnp.where(z_hi == 0, log_est[0:1], log_est[1:2])
+    flat = n_p - 1
+    wait_bytes(grad_p.at[0:flat], gp_sems.at[1])
+    share = grad_p[0]
+    for i in range(1, n_p):
+        share = share + grad_p[i]
     grad_z[z] = share
     for i in range(1, n_z):
         send(grad_z.at[z], gz_sems.at[0], gz_sems.at[1], at_z(i))
-    log_ref[...] = jnp.where(z_hi == 0, log_est[0:1], log_est[1:2])
+    table_copy.wait_send()
+    wait_bytes(pieces.at[0:flat], piece_sends.at[0])
+    wait_bytes(est.at[0 : n_z - 1], est_sems.at[0])
+    wait_bytes(grad_p.at[0:flat], gp_sems.at[0])
     wait_bytes(grad_z.at[0 : n_z - 1], gz_sems.at[1])
     share = grad_z[0]
     for i in range(1, n_z):
         share = share + grad_z[i]
-    grad_p[plane] = share
-    for i, j in plane_steps:
-        send(grad_p.at[plane], gp_sems.at[0], gp_sems.at[1], at_p(i, j))
-    table_copy.wait_send()
-    flat = n_p - 1
-    wait_bytes(pieces.at[0:flat], piece_sends.at[0])
-    wait_bytes(est.at[0 : n_z - 1], est_sems.at[0])
+    grad_ref[...] = share[:, :dims]
     wait_bytes(grad_z.at[0 : n_z - 1], gz_sems.at[0])
-    wait_bytes(grad_p.at[0:flat], gp_sems.at[1])
-    share = grad_p[0]
-    for i in range(1, n_p):
-        share = share + grad_p[i]
-    grad_ref[...] = share[:, :dims]
-    wait_bytes(grad_p.at[0:flat], gp_sems.at[0])
 
 
 def on_device(sizes, samples, bounds, spread, counts):
@@ -374,8 +381,17 @@
     sample_total = local * n_hi * n_y * n_a * n_lo
     query_total = queries * n_hi * n_y * n_a
     vmem = pl.BlockSpec(memory_space=pltpu.VMEM)
-    whole = pl.BlockSpec(memory_space=pl.ANY)
+    whole = pl.BlockSpec(memory_space=pltpu.HBM)
     dma = pltpu.SemaphoreType.DMA
+    inputs = [
+        pltpu.with_memory_space_constraint(value, pltpu.HBM)
+        for value in (
+            samples,
+            bounds,
+            spread.reshape(1, dims),
+            counts.reshape(1, queries),
+        )
+    ]
     log_est, grad = pl.pallas_call(
         functools.partial(kernel, sizes, float(sample_total), float(query_total)),
         out_shape=(
@@ -392,8 +408,7 @@
             pltpu.VMEM((n_hi, 16, 128), F32),
             pltpu.VMEM((n_y * n_a, 8, 128), F32),
             pltpu.VMEM((n_y, DEPTH, width), BF16),
-            pltpu.VMEM((n_hi, DEPTH, ROWS_PER_HALF), BF16),
-            pltpu.VMEM((ROWS_PER_HALF, width), F32),
+            pltpu.VMEM((n_hi, 128 // GROUP, 7 * GROUP, DEPTH), BF16),
             pltpu.VMEM((n_y, n_hi, 128, width), F32),
             pltpu.VMEM((n_y, dims, width), F32),
             pltpu.VMEM((4, n_hi, 128, 128), F32),
@@ -407,11 +422,12 @@
             dma((2,)),
             dma((2,)),
             dma((2,)),
+            pltpu.SemaphoreType.REGULAR,
         ],
         compiler_params=pltpu.CompilerParams(
             collective_id=0, has_side_effects=True, vmem_limit_bytes=40 * 1024 * 1024
         ),
-    )(samples, bounds, spread.reshape(1, dims), counts.reshape(1, queries))
+    )(*inputs)
     return log_est.reshape(queries), grad.reshape(dims)
 
 

time: 51.6 us -> 45.1 us (0.87)
  Pallas kernels: 47.5 us -> 43.3 us
  local copies, waits for them, and re-layouts: 3.15 us -> 1.02 us
    pallas_call x1, Pallas kernels: 47.5 us -> 43.3 us  [on_device(): pl.pallas_call(functools.partial(kernel, sizes, float(sample_total), floa...]
    unnamed x10 -> x2, local copies, waits for them, and re-layouts: 3.15 us -> 1.02 us
where the time goes in v3:
time: 45.1 us; the launch traced here: 45 us
  Pallas kernels  43.3 us (96%)
  local copies, waits for them, and re-layouts  1.02 us (2%)
  between operations  0.64 us (1%)
    pallas_call x1, Pallas kernels, on_device(): pl.pallas_call(functools.partial(kernel, sizes, float(sample_total), floa...  43.3 us
    unnamed x2, local copies, waits for them, and re-layouts  1.02 us

profile of v3, /device:TPU:1, one launch (start us, length us, event | category | flops | bytes accessed | tf_op | source)
XLA Modules:
  0.0 45.0 jit_solution(7196595115202057378)
XLA Ops:
  0.6 43.3 %shard_map.59 = (f32[1,128]{1,0:T(1,128)S(1)}, f32[1,32]{1,0:T(1,128)S(1)}) custom-call(f32[32,32]{1,0:T(8,128)} %samples_hbm.1, s32[2,32,128]{2,1,0:T(8,128)} %bounds_hbm.1, f32[1,32]{1,0:T(1,128)} %bitcast.6, s32[1,128]{1,0:T(1,128)} %bitcast.7), custom_call_target="tpu_custom_call" | custom-call | tf_op jit(solution)/shard_map/pallas_call | solution.py:395
  43.9 0.5 %copy.8 = f32[128]{0:T(128)} copy(f32[128]{0:T(128)S(1)} %bitcast.5) | data formatting | bytes 1024
  44.4 0.5 %copy.9 = f32[32]{0:T(128)} copy(f32[32]{0:T(128)S(1)} %bitcast.4) | data formatting | bytes 256

commit v4 on v3

--- a/solution.py
+++ b/solution.py
@@ -32,12 +32,16 @@
 DEPTH = 208
 
 
-def erf_and_moment(v):
+def erf_of(v):
     w = v * v
-    poly = jnp.full_like(w, ERF_COEFS[-1])
-    for coef in ERF_COEFS[-2::-1]:
+    poly = ERF_COEFS[-1] * w + ERF_COEFS[-2]
+    for coef in ERF_COEFS[-3::-1]:
         poly = poly * w + coef
-    return jnp.tanh(v * poly), v * jnp.exp2(-w)
+    return jnp.tanh(v * poly)
+
+
+def moment_of(v):
+    return v * jnp.exp2(-(v * v))
 
 
 def split3(x):
@@ -78,7 +82,7 @@
     rights,
     chosen,
     inside,
-    slopes,
+    leaves,
     sums,
     est,
     grad_z,
@@ -127,13 +131,18 @@
         return (z_hi * n_p + ((y + y_step) % n_y) * n_a + (a + a_step) % n_a, z_lo)
 
     partner = ((1 - z_hi) * n_p + plane, (z_lo + n_lo // 2) % n_lo)
-    plane_steps = [(i, j) for i in range(n_y) for j in range(n_a) if i or j]
+    plane_steps = sorted(
+        ((i, j) for i in range(n_y) for j in range(n_a) if i or j),
+        key=lambda s: -2 * min(s[0], n_y - s[0]) - min(s[1], n_a - s[1]),
+    )
+    z_steps = sorted(range(1, n_z), key=lambda i: -min(i, n_z - i))
 
     barrier = pltpu.get_barrier_semaphore()
-    peers = [at_p(i, j) for i, j in plane_steps]
-    near = [i for i in range(1, n_z) if min(i, n_z - i) <= REACH]
+    peers = []
+    near = [i for i in z_steps if min(i, n_z - i) <= REACH]
     hubs = [i for i in near if min(i, n_z - i) == REACH]
     peers += [at_z(i) for i in near]
+    peers += [at_p(i, j) for i, j in plane_steps]
     for peer in peers:
         pl.semaphore_signal(barrier, inc=1, device_id=peer, device_id_type=MESH)
 
@@ -197,8 +206,6 @@
     rows.append(jnp.zeros((6, 128), F32))
     table[z_hi] = jnp.concatenate(rows, axis=0)
     table_copy = send(table.at[z_hi], table_sems.at[0], table_sems.at[1], partner)
-
-    sums[...] = jnp.zeros_like(sums)
 
     def hot_rows(half):
         values = table[half]
@@ -236,7 +243,7 @@
     row = lax.broadcasted_iota(jnp.int32, (16, width), 0)
     ones = jnp.where(row < 3, 1.0, 0.0).astype(BF16)
 
-    def prepare(chunk):
+    def points_of(chunk):
         tiles = [pieces[chunk * n_a + i] for i in range(n_a)]
         points = jnp.concatenate(
             [
@@ -247,83 +254,107 @@
             ],
             axis=0,
         )
-        v_low = -points * inverse
-        v_high = float(GRID) * inverse + v_low
-        erf_high, moment_high = erf_and_moment(v_high)
-        erf_low, moment_low = erf_and_moment(v_low)
-        double_mass = erf_high - erf_low
-        slopes[chunk] = (moment_low - moment_high) / double_mass
-        logs = jnp.log(0.5 * double_mass) * LOG2E
-        rights[chunk] = jnp.concatenate(
-            list(split3(-v_low)) + list(split3(logs)) + [ones], axis=0
-        )
-
-    def block(step, carry):
-        i = step % n_y
-        chunk = (y + n_y - i) % n_y
-
-        @pl.when(step == 0)
-        def _():
-            wait_bytes(pieces.at[0 : n_a - 1], piece_recvs.at[i])
-
-        @pl.when((step > 0) & (step < n_y))
-        def _():
-            wait_bytes(pieces.at[0:n_a], piece_recvs.at[i])
-
-        @pl.when(step < n_y)
-        def _():
-            prepare(chunk)
-
-        @pl.when(step == n_y)
+        return points * inverse
+
+    def prepare(chunk):
+        point = points_of(chunk)
+        erf_high = erf_of(float(GRID) * inverse - point)
+        mass = 0.5 * (erf_high + erf_of(point))
+        logs = jnp.log(mass) * LOG2E
+        rights[:, chunk * width : chunk * width + width] = jnp.concatenate(
+            list(split3(point)) + list(split3(logs)) + [ones], axis=0
+        )
+
+    def slope_of(chunk):
+        point = points_of(chunk)
+        beyond = float(GRID) * inverse - point
+        return -(moment_of(point) + moment_of(beyond)) / (erf_of(beyond) + erf_of(point))
+
+    def arguments(half, group, chunk, rows):
+        terms = dot(
+            chosen[half, group, : rows * GROUP],
+            rights[:, chunk * width : chunk * width + width],
+            1,
+            0,
+        )
+        return [terms[n * GROUP : n * GROUP + GROUP] for n in range(rows)]
+
+    def fold(part):
+        total = part[:, :128]
+        for j in range(1, width // 128):
+            total = total + part[:, 128 * j : 128 * j + 128]
+        return total
+
+    def masses_of(half):
+        for group in range(128 // GROUP):
+            here = slice(group * GROUP, group * GROUP + GROUP)
+            total = None
+            for chunk in range(n_y):
+                terms = arguments(half, group, chunk, 7)
+                first, second, third = (
+                    erf_of(terms[2 * k]) - erf_of(terms[2 * k + 1]) for k in range(3)
+                )
+                rest = jnp.exp2(terms[6])
+                rest0 = rest * first
+                rest01 = rest0 * second
+                within = rest01 * third
+                inside[chunk, half, here, :] = within
+                leaves[0, chunk, half, here, :] = rest * (second * third)
+                leaves[1, chunk, half, here, :] = rest0 * third
+                leaves[2, chunk, half, here, :] = rest01
+                part = fold(within)
+                total = part if total is None else total + part
+            sums[0, half, here, :] = total
+
+    def moments_of(half):
+        for group in range(128 // GROUP):
+            here = slice(group * GROUP, group * GROUP + GROUP)
+            totals = [None] * 3
+            for chunk in range(n_y):
+                terms = arguments(half, group, chunk, 6)
+                for k in range(3):
+                    moment = moment_of(terms[2 * k + 1]) - moment_of(terms[2 * k])
+                    part = fold(leaves[k, chunk, half, here, :] * moment)
+                    totals[k] = part if totals[k] is None else totals[k] + part
+            for k in range(3):
+                sums[k + 1, half, here, :] = totals[k]
+
+    for i in range(n_y):
+        count = n_a - 1 if i == 0 else n_a
+        wait_bytes(pieces.at[0:count], piece_recvs.at[i])
+    for chunk in range(n_y):
+        prepare(chunk)
+
+    def half_block(step, carry):
+        @pl.when(step == 1)
         def _():
             table_copy.wait_recv()
             choose(1 - z_hi)
 
-        half = jnp.where(step < n_y, z_hi, 1 - z_hi)
-        right = rights[chunk]
-        for group in range(128 // GROUP):
-            terms = dot(chosen[half, group], right, 1, 0)
-            terms = [terms[n * GROUP : n * GROUP + GROUP] for n in range(7)]
-            start = group * GROUP
-            masses, moments = [], []
-            for k in range(3):
-                erf_high, moment_high = erf_and_moment(terms[2 * k])
-                erf_low, moment_low = erf_and_moment(terms[2 * k + 1])
-                masses.append(erf_high - erf_low)
-                moments.append(moment_low - moment_high)
-            rest = jnp.exp2(terms[6])
-            rest0 = rest * masses[0]
-            rest01 = rest0 * masses[1]
-            within = rest01 * masses[2]
-            inside[chunk, half, start : start + GROUP, :] = within
-            parts = [
-                within,
-                rest * (masses[1] * masses[2]) * moments[0],
-                rest0 * masses[2] * moments[1],
-                rest01 * moments[2],
-            ]
-            for n, part in enumerate(parts):
-                folded = part[:, :128]
-                for j in range(1, width // 128):
-                    folded = folded + part[:, 128 * j : 128 * j + 128]
-                sums[n, half, start : start + GROUP, :] += folded
+        masses_of(jnp.where(step == 0, z_hi, 1 - z_hi))
         return carry
 
-    lax.fori_loop(0, n_hi * n_y, block, 0)
+    lax.fori_loop(0, n_hi, half_block, 0)
 
     for half in range(n_hi):
         est[z, half : half + 1] = row_sums(sums[0, half])
     if hubs:
         pl.semaphore_wait(ready, len(hubs))
-    for i in range(1, n_z):
+    for i in z_steps:
         send(est.at[z], est_sems.at[0], est_sems.at[1], at_z(i))
+    def half_moments(half, carry):
+        moments_of(half)
+        return carry
+
+    lax.fori_loop(0, n_hi, half_moments, 0)
     derivs = []
+    slopes = [split3(slope_of(chunk)) for chunk in range(n_y)]
     for half in range(n_hi):
         hots = hot_rows(half)
         free = 1.0 - (hots[0] + hots[1] + hots[2])
         total = jnp.zeros((dims, 128), F32)
         for chunk in range(n_y):
-            steep, steep_rest, _ = split3(slopes[chunk])
+            steep, steep_rest, _ = slopes[chunk]
             within, within_rest, _ = split3(inside[chunk, half])
             total = total + dot(steep, within, 1, 1)
             total = total + dot(steep_rest, within, 1, 1)
@@ -358,7 +389,7 @@
     for i in range(1, n_p):
         share = share + grad_p[i]
     grad_z[z] = share
-    for i in range(1, n_z):
+    for i in z_steps:
         send(grad_z.at[z], gz_sems.at[0], gz_sems.at[1], at_z(i))
     table_copy.wait_send()
     wait_bytes(pieces.at[0:flat], piece_sends.at[0])
@@ -407,10 +438,10 @@
             pltpu.VMEM((1, queries), jnp.int32),
             pltpu.VMEM((n_hi, 16, 128), F32),
             pltpu.VMEM((n_y * n_a, 8, 128), F32),
-            pltpu.VMEM((n_y, DEPTH, width), BF16),
+            pltpu.VMEM((DEPTH, n_y * width), BF16),
             pltpu.VMEM((n_hi, 128 // GROUP, 7 * GROUP, DEPTH), BF16),
             pltpu.VMEM((n_y, n_hi, 128, width), F32),
-            pltpu.VMEM((n_y, dims, width), F32),
+            pltpu.VMEM((3, n_y, n_hi, 128, width), F32),
             pltpu.VMEM((4, n_hi, 128, 128), F32),
             pltpu.VMEM((n_z, n_hi, 128), F32),
             pltpu.VMEM((n_z, 1, 128), F32),

time: 45.1 us -> 43.8 us (0.971)
  Pallas kernels: 43.3 us -> 42 us
    pallas_call x1, Pallas kernels: 43.3 us -> 42 us  [on_device(): pl.pallas_call(functools.partial(kernel, sizes, float(sample_total), floa...]
where the time goes in v4:
time: 43.8 us; the launch traced here: 43.7 us
  Pallas kernels  42 us (96%)
  local copies, waits for them, and re-layouts  1.02 us (2%)
  between operations  0.64 us (1%)
    pallas_call x1, Pallas kernels, on_device(): pl.pallas_call(functools.partial(kernel, sizes, float(sample_total), floa...  42 us
    unnamed x2, local copies, waits for them, and re-layouts  1.02 us

profile of v4, /device:TPU:1, one launch (start us, length us, event | category | flops | bytes accessed | tf_op | source)
XLA Modules:
  0.0 43.7 jit_solution(3851176091672948284)
XLA Ops:
  0.6 42.0 %shard_map.59 = (f32[1,128]{1,0:T(1,128)S(1)}, f32[1,32]{1,0:T(1,128)S(1)}) custom-call(f32[32,32]{1,0:T(8,128)} %samples_hbm.1, s32[2,32,128]{2,1,0:T(8,128)} %bounds_hbm.1, f32[1,32]{1,0:T(1,128)} %bitcast.6, s32[1,128]{1,0:T(1,128)} %bitcast.7), custom_call_target="tpu_custom_call" | custom-call | tf_op jit(solution)/shard_map/pallas_call | solution.py:426
  42.6 0.5 %copy.8 = f32[128]{0:T(128)} copy(f32[128]{0:T(128)S(1)} %bitcast.5) | data formatting | bytes 1024
  43.2 0.5 %copy.9 = f32[32]{0:T(128)} copy(f32[32]{0:T(128)S(1)} %bitcast.4) | data formatting | bytes 256

commit v5 on v4

--- a/solution.py
+++ b/solution.py
@@ -27,7 +27,7 @@
 SLOPE_SCALE = 2.0 / (math.sqrt(2.0 * math.pi) * UNIT)
 
 GRID = 256
-GROUP = 16
+GROUP = 32
 REACH = 4
 DEPTH = 208
 
@@ -166,12 +166,6 @@
     pieces[plane] = jnp.concatenate(
         [x[8 * i : 8 * i + 8] for i in range(dims // 8)], axis=1
     )
-    pl.semaphore_wait(barrier, len(peers))
-    for i in hubs:
-        pl.semaphore_signal(ready, inc=1, device_id=at_z(i), device_id_type=MESH)
-    for i, j in plane_steps:
-        send(pieces.at[plane], piece_sends.at[0], piece_recvs.at[i], at_p(i, j))
-
     inputs[1].wait()
     inverse = UNIT / spread_ref[...]
     eye = lax.broadcasted_iota(jnp.int32, (dims, dims), 0) == lax.broadcasted_iota(
@@ -205,8 +199,6 @@
     rows.append(counts_ref[...].astype(F32))
     rows.append(jnp.zeros((6, 128), F32))
     table[z_hi] = jnp.concatenate(rows, axis=0)
-    table_copy = send(table.at[z_hi], table_sems.at[0], table_sems.at[1], partner)
-
     def hot_rows(half):
         values = table[half]
         return [
@@ -240,11 +232,20 @@
                 ]
 
     choose(z_hi)
+
+    pl.semaphore_wait(barrier, len(peers))
+    table_copy = send(table.at[z_hi], table_sems.at[0], table_sems.at[1], partner)
+    for i, j in plane_steps:
+        send(pieces.at[plane], piece_sends.at[0], piece_recvs.at[i], at_p(i, j))
+    for i in hubs:
+        pl.semaphore_signal(ready, inc=1, device_id=at_z(i), device_id_type=MESH)
+
     row = lax.broadcasted_iota(jnp.int32, (16, width), 0)
     ones = jnp.where(row < 3, 1.0, 0.0).astype(BF16)
 
     def points_of(chunk):
-        tiles = [pieces[chunk * n_a + i] for i in range(n_a)]
+        first = ((y + n_y - chunk) % n_y) * n_a
+        tiles = [pieces[first + i] for i in range(n_a)]
         points = jnp.concatenate(
             [
                 jnp.concatenate(
@@ -286,10 +287,11 @@
         return total
 
     def masses_of(half):
-        for group in range(128 // GROUP):
-            here = slice(group * GROUP, group * GROUP + GROUP)
-            total = None
-            for chunk in range(n_y):
+        groups = range(128 // GROUP)
+        totals = [None for _ in groups]
+        for chunk in range(n_y):
+            for group in groups:
+                here = slice(group * GROUP, group * GROUP + GROUP)
                 terms = arguments(half, group, chunk, 7)
                 first, second, third = (
                     erf_of(terms[2 * k]) - erf_of(terms[2 * k + 1]) for k in range(3)
@@ -303,8 +305,9 @@
                 leaves[1, chunk, half, here, :] = rest0 * third
                 leaves[2, chunk, half, here, :] = rest01
                 part = fold(within)
-                total = part if total is None else total + part
-            sums[0, half, here, :] = total
+                totals[group] = part if chunk == 0 else totals[group] + part
+        for group in groups:
+            sums[0, half, group * GROUP : group * GROUP + GROUP, :] = totals[group]
 
     def moments_of(half):
         for group in range(128 // GROUP):
@@ -322,8 +325,7 @@
     for i in range(n_y):
         count = n_a - 1 if i == 0 else n_a
         wait_bytes(pieces.at[0:count], piece_recvs.at[i])
-    for chunk in range(n_y):
-        prepare(chunk)
+        prepare(i)
 
     def half_block(step, carry):
         @pl.when(step == 1)
@@ -336,8 +338,9 @@
 
     lax.fori_loop(0, n_hi, half_block, 0)
 
+    totals = row_sums(jnp.concatenate([sums[0, half] for half in range(n_hi)], axis=0))
     for half in range(n_hi):
-        est[z, half : half + 1] = row_sums(sums[0, half])
+        est[z, half : half + 1] = totals[:, 128 * half : 128 * half + 128]
     if hubs:
         pl.semaphore_wait(ready, len(hubs))
     for i in z_steps:

time: 43.8 us -> 43.4 us (level)
  Pallas kernels: 42 us -> 41.5 us
    pallas_call x1, Pallas kernels: 42 us -> 41.5 us  [on_device(): pl.pallas_call(functools.partial(kernel, sizes, float(sample_total), floa...]
where the time goes in v5:
time: 43.4 us; the launch traced here: 43.2 us
  Pallas kernels  41.5 us (96%)
  local copies, waits for them, and re-layouts  1.02 us (2%)
  between operations  0.64 us (1%)
    pallas_call x1, Pallas kernels, on_device(): pl.pallas_call(functools.partial(kernel, sizes, float(sample_total), floa...  41.5 us
    unnamed x2, local copies, waits for them, and re-layouts  1.02 us

profile of v5, /device:TPU:1, one launch (start us, length us, event | category | flops | bytes accessed | tf_op | source)
XLA Modules:
  0.0 43.2 jit_solution(7224328124520234485)
XLA Ops:
  0.6 41.5 %shard_map.59 = (f32[1,128]{1,0:T(1,128)S(1)}, f32[1,32]{1,0:T(1,128)S(1)}) custom-call(f32[32,32]{1,0:T(8,128)} %samples_hbm.1, s32[2,32,128]{2,1,0:T(8,128)} %bounds_hbm.1, f32[1,32]{1,0:T(1,128)} %bitcast.6, s32[1,128]{1,0:T(1,128)} %bitcast.7), custom_call_target="tpu_custom_call" | custom-call | tf_op jit(solution)/shard_map/pallas_call | solution.py:429
  42.2 0.5 %copy.8 = f32[128]{0:T(128)} copy(f32[128]{0:T(128)S(1)} %bitcast.5) | data formatting | bytes 1024
  42.7 0.5 %copy.9 = f32[32]{0:T(128)} copy(f32[32]{0:T(128)S(1)} %bitcast.4) | data formatting | bytes 256

commit v6 on v5

--- a/solution.py
+++ b/solution.py
@@ -27,7 +27,7 @@
 SLOPE_SCALE = 2.0 / (math.sqrt(2.0 * math.pi) * UNIT)
 
 GRID = 256
-GROUP = 32
+GROUP = 128
 REACH = 4
 DEPTH = 208
 

time: 43.4 us -> 43.3 us (level)
  no operation moved by 1% of the time
where the time goes in v6:
time: 43.3 us; the launch traced here: 43.1 us
  Pallas kernels  41.5 us (96%)
  local copies, waits for them, and re-layouts  1.02 us (2%)
  between operations  0.64 us (1%)
    pallas_call x1, Pallas kernels, on_device(): pl.pallas_call(functools.partial(kernel, sizes, float(sample_total), floa...  41.5 us
    unnamed x2, local copies, waits for them, and re-layouts  1.02 us

profile of v6, /device:TPU:1, one launch (start us, length us, event | category | flops | bytes accessed | tf_op | source)
XLA Modules:
  0.0 43.1 jit_solution(11458493032024910782)
XLA Ops:
  0.6 41.5 %shard_map.59 = (f32[1,128]{1,0:T(1,128)S(1)}, f32[1,32]{1,0:T(1,128)S(1)}) custom-call(f32[32,32]{1,0:T(8,128)} %samples_hbm.1, s32[2,32,128]{2,1,0:T(8,128)} %bounds_hbm.1, f32[1,32]{1,0:T(1,128)} %bitcast.6, s32[1,128]{1,0:T(1,128)} %bitcast.7), custom_call_target="tpu_custom_call" | custom-call | tf_op jit(solution)/shard_map/pallas_call | solution.py:429
  42.1 0.5 %copy.8 = f32[128]{0:T(128)} copy(f32[128]{0:T(128)S(1)} %bitcast.5) | data formatting | bytes 1024
  42.6 0.5 %copy.9 = f32[32]{0:T(128)} copy(f32[32]{0:T(128)S(1)} %bitcast.4) | data formatting | bytes 256
